TPU v7x, 32 devices: a whole 2x2x4 slice. The times are simulated.
32 devices in a mesh: row: 8 (over y, x, core), col: 4 (over z).
Axes of the slice: x: 2, y: 2, z: 4, core: 2. Of those that a mesh axis runs over, the one named last changes fastest.
Arguments:
- inverse_blocks: float32 [4096, 4096], P('row', 'col'), may hold values from -0.09375 to 0.09375
- panel: bfloat16 [4096, 4096], P('row', 'col'), may hold values from -1.5 to 1.5
- diag_inverse: float32 [512, 4096], P('row', 'col'), may hold values from -6 to 6
- members: int32 [8, 8], replicated, may hold values from 0 to 7, each once within a row
- counts: int32 [8], replicated, may hold values from 1 to 8, as said below
Outputs:
- offdiag: float32 [4096, 4096], P('row', 'col')
- new_diag: float32 [512, 4096], P('row', 'col')
Inputs may be any that keep to these rules, and one draw needn't show every extreme that they name: Each row of members names every ancestor once. `counts`: some supernode lists all 8 ancestors and some lists one.
All inputs are finite; a program needn't handle non-finite values.
Results may differ from a plain program's by a relative error of at most 0.0003.
Values may be sent and summed in bfloat16 or wider, within the bound.
A program may use at most 128 MiB of HBM per device.

v0:
```python
import jax
import jax.numpy as jnp
from jax import lax
from jax.sharding import PartitionSpec as P

B = 512


def body(inverse_blocks, panel, diag_inverse, members, counts):
    rows_dev = panel.shape[0]
    sup_count = panel.shape[1] // B
    row_index = lax.axis_index("row")
    col_index = lax.axis_index("col")
    ancestor = row_index * rows_dev // B
    first_sup = col_index * sup_count
    local_members = lax.dynamic_slice_in_dim(members, first_sup, sup_count, 0)
    local_counts = lax.dynamic_slice_in_dim(counts, first_sup, sup_count, 0)
    slot_index = jnp.arange(members.shape[1], dtype=jnp.int32)
    live_slot = slot_index[None, :] < local_counts[:, None]
    row_mask = jnp.sum(
        jnp.where((local_members == ancestor) & live_slot, 1.0, 0.0).astype(jnp.float32), axis=1
    )
    column_mask = jnp.repeat(row_mask, B)
    masked = panel * column_mask.astype(jnp.bfloat16)[None, :]
    inverse_rows = lax.all_gather(inverse_blocks, "col", axis=1, tiled=True)
    running = jnp.dot(
        inverse_rows,
        lax.all_gather(masked, "row", axis=0, tiled=True).astype(jnp.float32),
        precision=lax.Precision.HIGHEST,
    )
    offdiag = -(running * column_mask[None, :])
    masked_wide = masked.astype(jnp.float32).reshape(rows_dev, sup_count, B)
    offdiag_wide = offdiag.reshape(rows_dev, sup_count, B)
    diag_terms = jnp.einsum(
        "ikc,ikd->ckd", masked_wide, offdiag_wide, precision=lax.Precision.HIGHEST
    )
    summed = lax.psum_scatter(
        diag_terms.reshape(B, sup_count * B), "row", scatter_dimension=0, tiled=True
    )
    return (offdiag, diag_inverse - summed)


def solution(mesh):
    return jax.shard_map(
        body,
        mesh=mesh,
        in_specs=(P("row", "col"), P("row", "col"), P("row", "col"), P(), P()),
        out_specs=(P("row", "col"), P("row", "col")),
        check_vma=False,
    )
```

profile of v0, /device:TPU:0, one launch (start us, length us, event | category | flops | bytes accessed | tf_op | source)
XLA Modules:
  0.0 291.6 jit_solution(4853133798508175931)
XLA Ops:
  7.2 0.0 copy-start.3
  7.2 0.0 copy-start.1
  7.2 0.0 all-gather.5.cloned.1.call-start
  7.2 0.7 all-gather.5.cloned.1.call-update
  7.9 0.0 all-gather.3.cloned.1.call-start
  8.0 0.0 copy-done.3
  8.0 0.1 dynamic_slice.7
  8.1 0.9 fusion.3
  8.9 0.1 broadcast_bitcast_fusion
  9.0 0.0 copy-done.1
  9.0 1.0 broadcast_multiply_fusion
  10.1 0.0 all-gather.3.cloned.1.call-update
  10.1 0.0 copy-start
  10.1 0.0 reduce-scatter.2.cloned.1.call-start
  10.2 151.8 %all-gather.5.cloned.1.call-done = f32[512,4096]{1,0:T(8,128)} async-done(((f32[512,1024]{1,0:T(8,128)}), f32[512,4096]{1,0:T(8,128)}) %all-gather.5.cloned.1.call-update) | async-done | bytes 8388624 | tf_op jit(solution)/shard_map/all_gather | solution.py:25
  162.0 55.1 %all-gather.3.cloned.1.call-done = bf16[4096,1024]{1,0:T(8,128)(2,1)} async-done(((bf16[512,1024]{1,0:T(8,128)(2,1)}), bf16[4096,1024]{1,0:T(8,128)(2,1)}) %all-gather.3.cloned.1.call-update) | async-done | bytes 8388624 | tf_op jit(solution)/shard_map/all_gather | solution.py:28
  217.0 18.9 %multiply_negate_fusion = f32[1024,512]{1,0:T(8,128)S(1)} fusion(bf16[4096,1024]{1,0:T(8,128)(2,1)} %all-gather.3.cloned.1.call-done, f32[512,4096]{1,0:T(8,128)} %all-gather.5.cloned.1.call-done, f32[1024]{0:T(1024)S(1)} %bitcast.21), kind=kOutput, calls=%fused_computation | convolution fusion | flops 25770852352 | bytes 18878464 | tf_op jit(solution)/shard_map/dot_general | solution.py:26
  235.9 0.0 copy-done
  235.9 3.1 %fusion = f32[2,512,512]{2,1,0:T(8,128)} fusion(f32[512,2,512]{0,2,1:T(8,128)S(1)} %bitcast.17, bf16[64,2,8,512]{3,2,1,0:T(8,128)(2,1)S(1)} %bitcast.16), kind=kOutput, calls=%fused_computation.1 | convolution fusion | flops 3221225472 | bytes 5242880 | tf_op jit(solution)/shard_map/ikc,ikd->ckd/dot_general | solution.py:34
  239.0 2.9 %copy.8 = f32[512,1024]{1,0:T(8,128)} copy(f32[512,1024]{0,1:T(8,128)} %bitcast.19) | data formatting | bytes 4194304 | tf_op jit(solution)/shard_map/reshape | solution.py:38
  242.0 0.0 reduce-scatter.2.cloned.1.call-update
  242.0 0.0 copy-start.2
  242.0 1.8 copy.9
  243.8 39.6 %reduce-scatter.2.cloned.1.call-done = f32[64,1024]{1,0:T(8,128)} async-done(((f32[512,1024]{1,0:T(8,128)}), f32[64,1024]{1,0:T(8,128)}) %reduce-scatter.2.cloned.1.call-update) | async-done | bytes 262160 | tf_op jit(solution)/shard_map/reduce_scatter | solution.py:37
  283.4 0.0 copy-done.2
  283.4 1.7 sub.8
  (2 shorter events, 0.0 us)
Async XLA Ops:
  7.2 0.8 copy-start.3
  7.2 1.9 copy-start.1
  7.2 154.8 %all-gather.5.cloned.1.call-start = ((), (), s32[]{:S(2)}) async-start(), calls=%async_computation.2 | async-start | bytes 10485760 | tf_op jit(solution)/shard_map/all_gather | solution.py:25
  7.9 209.1 %all-gather.3.cloned.1.call-start = ((), (), s32[]{:S(2)}) async-start(), calls=%async_computation.1 | async-start | bytes 9437184 | tf_op jit(solution)/shard_map/all_gather | solution.py:28
  10.1 225.8 %copy-start = (bf16[512,1024]{1,0:T(8,128)(2,1)S(1)}, bf16[512,1024]{1,0:T(8,128)(2,1)}, u32[]{:S(2)}) copy-start(bf16[512,1024]{1,0:T(8,128)(2,1)} %broadcast_multiply_fusion) | copy-start | bytes 3145732
  10.1 273.3 %reduce-scatter.2.cloned.1.call-start = ((), (), s32[]{:S(2)}) async-start(), calls=%async_computation.3 | async-start | bytes 2359296 | tf_op jit(solution)/shard_map/reduce_scatter | solution.py:37
  242.0 41.4 %copy-start.2 = (f32[64,1024]{1,0:T(8,128)S(1)}, f32[64,1024]{1,0:T(8,128)}, u32[]{:S(2)}) copy-start(f32[64,1024]{1,0:T(8,128)} %param.7) | copy-start | bytes 786436
Sparse Core Ops, SparseCore 0:
  9.6 152.3 all-gather.4
  164.4 52.5 all-gather.2
  242.1 41.2 reduce-scatter.1
where the time goes:
time: 292 us
  waiting for transfers between devices  247 us (85%)
  matrix products  22 us (8%)
  between operations  13.8 us (5%)
  local copies, waits for them, and re-layouts  4.93 us (2%)
  other arithmetic  3.6 us (1%)
    all_gather x1, waiting for transfers between devices, body(): inverse_rows = lax.all_gather(inverse_blocks, 'col', axis=1, tiled=True)  152 us
    all_gather x1, waiting for transfers between devices, body(): lax.all_gather(masked, 'row', axis=0, tiled=True).astype(jnp.float32)  55.1 us
    reduce_scatter x1, waiting for transfers between devices, body(): lax.psum_scatter(diag_terms.reshape(B, sup_count * B), 'row', scatter_dim...  39.6 us
    dot_general x1, matrix products, body(): jnp.dot(inverse_rows, lax.all_gather(masked, 'row', axis=0, tiled=True).a...  18.9 us
  transfers between devices with their start and end apart: 3, of which 3 were waited for; matrix products, arithmetic and copies ran while one was open for 1% of the time, Pallas kernels for 0%

commit v1 on v0

--- a/solution.py
+++ b/solution.py
@@ -4,6 +4,19 @@
 from jax.sharding import PartitionSpec as P
 
 B = 512
+
+
+def collect(x, axis, dim):
+    ways = lax.axis_size(axis)
+    up = [(d, (d + 1) % ways) for d in range(ways)]
+    down = [(d, (d - 1) % ways) for d in range(ways)]
+    earlier, later = ([x], [x])
+    for _ in range(ways // 2):
+        earlier.append(lax.ppermute(earlier[-1], axis, up))
+    for _ in range((ways - 1) // 2):
+        later.append(lax.ppermute(later[-1], axis, down))
+    line = jnp.concatenate([*earlier[::-1], *later[1:]], axis=dim)
+    return jnp.roll(line, (lax.axis_index(axis) - ways // 2) * x.shape[dim], axis=dim)
 
 
 def body(inverse_blocks, panel, diag_inverse, members, counts):
@@ -24,9 +37,7 @@
     masked = panel * column_mask.astype(jnp.bfloat16)[None, :]
     inverse_rows = lax.all_gather(inverse_blocks, "col", axis=1, tiled=True)
     running = jnp.dot(
-        inverse_rows,
-        lax.all_gather(masked, "row", axis=0, tiled=True).astype(jnp.float32),
-        precision=lax.Precision.HIGHEST,
+        inverse_rows, collect(masked, "row", 0).astype(jnp.float32), precision=lax.Precision.HIGHEST
     )
     offdiag = -(running * column_mask[None, :])
     masked_wide = masked.astype(jnp.float32).reshape(rows_dev, sup_count, B)

time: 292 us -> 236 us (0.81)
  waiting for transfers between devices: 247 us -> 153 us
  local copies, waits for them, and re-layouts: 4.93 us -> 30 us
  starting transfers between devices: 0.12 us -> 7.84 us
  other arithmetic: 3.6 us -> 7.58 us
    all_gather x1, waiting for transfers between devices: 152 us -> 32.1 us  [body(): inverse_rows = lax.all_gather(inverse_blocks, 'col', axis=1, tiled=True)]
    ppermute x0 -> x7, waiting for transfers between devices: none -> 82.9 us  [the longest x4 82.9 us: collect(): earlier.append(lax.ppermute(earlier[-1], axis, up))]
    all_gather x1 -> x0, waiting for transfers between devices: 55.1 us -> none  [body(): lax.all_gather(masked, 'row', axis=0, tiled=True).astype(jnp.float32)]
    unnamed x11 -> x28, local copies, waits for them, and re-layouts: 1.91 us -> 25.3 us
    ppermute x0 -> x7, starting transfers between devices: none -> 7.76 us  [the longest x3 7.25 us: collect(): later.append(lax.ppermute(later[-1], axis, down))]
    unnamed x0 -> x2, other arithmetic: none -> 3.73 us
  transfers between devices with their start and end apart: 3 -> 9, of which waited for: 3 -> 6; matrix products, arithmetic and copies ran while one was open for 1% -> 14% of each run, Pallas kernels for 0% -> 0%
where the time goes in v1:
time: 236 us; the launch traced here: 235 us
  waiting for transfers between devices  153 us (65%)
  local copies, waits for them, and re-layouts  30 us (13%)
  matrix products  22 us (9%)
  between operations  14.1 us (6%)
  starting transfers between devices  7.84 us (3%)
  other arithmetic  7.58 us (3%)
    ppermute x4, waiting for transfers between devices, collect(): earlier.append(lax.ppermute(earlier[-1], axis, up))  82.9 us
    reduce_scatter x1, waiting for transfers between devices, body(): lax.psum_scatter(diag_terms.reshape(B, sup_count * B), 'row', scatter_dim...  37.8 us
    all_gather x1, waiting for transfers between devices, body(): inverse_rows = lax.all_gather(inverse_blocks, 'col', axis=1, tiled=True)  32.1 us
    unnamed x28, local copies, waits for them, and re-layouts  25.3 us
    dot_general x1, matrix products, body(): jnp.dot(inverse_rows, collect(masked, 'row', 0).astype(jnp.float32), prec...  18.9 us
    ppermute x3, starting transfers between devices, collect(): later.append(lax.ppermute(later[-1], axis, down))  7.25 us
  transfers between devices with their start and end apart: 9, of which 6 were waited for; matrix products, arithmetic and copies ran while one was open for 14% of the time, Pallas kernels for 0%

profile of v1, /device:TPU:0, one launch (start us, length us, event | category | flops | bytes accessed | tf_op | source)
XLA Modules:
  0.0 235.0 jit_solution(14626788491708903919)
XLA Ops:
  7.2 0.0 copy-start
  7.2 0.0 all-gather.2.cloned.1.call-start
  7.2 0.7 all-gather.2.cloned.1.call-update
  7.9 0.0 reduce-scatter.2.cloned.1.call-start
  8.0 0.7 dynamic_slice.11
  8.7 0.9 fusion.7
  9.6 0.1 broadcast_bitcast_fusion
  9.7 1.3 broadcast_multiply_fusion
  11.0 0.0 copy-start.1
  11.0 0.5 collective-permute-start
  11.5 15.4 %collective-permute-done = bf16[512,1024]{1,0:T(8,128)(2,1)S(1)} collective-permute-done((bf16[512,1024]{1,0:T(8,128)(2,1)S(1)}, bf16[512,1024]{1,0:T(8,128)(2,1)S(1)}, u32[]{:S(2)}, u32[]{:S(2)}) %collective-permute-start) | collective-permute-done | bytes 1048608 | tf_op jit(solution)/shard_map/ppermute | solution.py:15
  26.8 0.0 collective-permute-start.1
  26.8 0.0 copy-done.1
  26.8 2.6 %collective-permute-start.4 = (bf16[512,1024]{1,0:T(8,128)(2,1)S(1)}, bf16[512,1024]{1,0:T(8,128)(2,1)S(1)}, u32[]{:S(2)}, u32[]{:S(2)}) collective-permute-start(bf16[512,1024]{1,0:T(8,128)(2,1)S(1)} %broadcast_multiply_fusion), channel_id=1, source_target_pairs={{0,28},{4,0},{8,4},{12,8},{16,12},{20,16},{24,20},{28,24},{1,29},{... | collective-permute-start | bytes 3145736 | tf_op jit(solution)/shard_map/ppermute | solution.py:17
  29.5 21.9 %collective-permute-done.1 = bf16[512,1024]{1,0:T(8,128)(2,1)S(1)} collective-permute-done((bf16[512,1024]{1,0:T(8,128)(2,1)S(1)}, bf16[512,1024]{1,0:T(8,128)(2,1)S(1)}, u32[]{:S(2)}, u32[]{:S(2)}) %collective-permute-start.1) | collective-permute-done | bytes 1048608 | tf_op jit(solution)/shard_map/ppermute | solution.py:15
  51.4 0.0 copy-start.3
  51.4 0.0 collective-permute-start.2
  51.4 0.0 collective-permute-done.4
  51.4 1.0 copy-done.3
  52.4 2.0 collective-permute-start.5
  54.4 22.2 %collective-permute-done.2 = bf16[512,1024]{1,0:T(8,128)(2,1)} collective-permute-done((bf16[512,1024]{1,0:T(8,128)(2,1)S(1)}, bf16[512,1024]{1,0:T(8,128)(2,1)}, u32[]{:S(2)}, u32[]{:S(2)}) %collective-permute-start.2) | collective-permute-done | bytes 1048608 | tf_op jit(solution)/shard_map/ppermute | solution.py:15
  76.6 0.0 collective-permute-start.3
  76.6 0.0 copy-start.4
  76.6 0.0 collective-permute-done.5
  76.6 2.6 %collective-permute-start.6 = (bf16[512,1024]{1,0:T(8,128)(2,1)}, bf16[512,1024]{1,0:T(8,128)(2,1)S(1)}, u32[]{:S(2)}, u32[]{:S(2)}) collective-permute-start(bf16[512,1024]{1,0:T(8,128)(2,1)} %collective-permute-done.5), channel_id=1, source_target_pairs={{0,28},{4,0},{8,4},{12,8},{16,12},{20,16},{24,20},{28,24},{1,29},{... | collective-permute-start | bytes 3145736 | tf_op jit(solution)/shard_map/ppermute | solution.py:17
  79.2 23.4 %collective-permute-done.3 = bf16[512,1024]{1,0:T(8,128)(2,1)} collective-permute-done((bf16[512,1024]{1,0:T(8,128)(2,1)}, bf16[512,1024]{1,0:T(8,128)(2,1)}, u32[]{:S(2)}, u32[]{:S(2)}) %collective-permute-start.3) | collective-permute-done | bytes 1048608 | tf_op jit(solution)/shard_map/ppermute | solution.py:15
  102.6 2.3 constant_dynamic-update-slice_fusion.15
  104.9 2.3 constant_dynamic-update-slice_fusion.14
  107.2 2.3 constant_dynamic-update-slice_fusion.13
  109.4 1.1 constant_dynamic-update-slice_fusion.12
  110.5 2.4 %constant_dynamic-update-slice_fusion.11 = bf16[8192,1024]{1,0:T(8,128)(2,1)} fusion(bf16[8192,1024]{1,0:T(8,128)(2,1)} %constant_dynamic-update-slice_fusion.12, bf16[512,1024]{1,0:T(8,128)(2,1)} %param.6, bf16[1024]{0:T(1024)(128)(2,1)S(1)} %convert_element_type.9), kind=kLoop, calls=%fused_computation.18 | loop fusion | flops 2097152 | bytes 2099200
  112.9 1.1 constant_dynamic-update-slice_fusion.10
  114.0 2.3 constant_dynamic-update-slice_fusion.9
  116.3 0.0 collective-permute-done.6
  116.3 1.1 constant_dynamic-update-slice_fusion.8
  117.4 2.4 %constant_dynamic-update-slice_fusion.7 = bf16[8192,1024]{1,0:T(8,128)(2,1)} fusion(bf16[8192,1024]{1,0:T(8,128)(2,1)} %constant_dynamic-update-slice_fusion.8, bf16[512,1024]{1,0:T(8,128)(2,1)} %collective-permute-done.3), kind=kLoop, calls=%fused_computation.14 | loop fusion | bytes 2097152
  119.8 2.3 constant_dynamic-update-slice_fusion.6
  122.0 0.0 copy-done.4
  122.0 1.1 constant_dynamic-update-slice_fusion.5
  123.1 1.1 constant_dynamic-update-slice_fusion.4
  124.2 0.0 copy-done
  124.2 1.3 constant_dynamic-update-slice_fusion.3
  125.5 1.1 constant_dynamic-update-slice_fusion.2
  126.5 2.3 constant_dynamic-update-slice_fusion.1
  128.8 0.0 copy-start.2
  128.8 1.0 constant_dynamic-update-slice_fusion
  129.8 0.0 copy-start.5
  129.8 32.1 %all-gather.2.cloned.1.call-done = f32[512,4096]{1,0:T(8,128)} async-done(((f32[512,1024]{1,0:T(8,128)}), f32[512,4096]{1,0:T(8,128)}) %all-gather.2.cloned.1.call-update) | async-done | bytes 8388624 | tf_op jit(solution)/shard_map/all_gather | solution.py:38
  162.0 18.9 %multiply_negate_fusion = f32[1024,512]{1,0:T(8,128)S(1)} fusion(f32[512,4096]{1,0:T(8,128)} %all-gather.2.cloned.1.call-done, bf16[8192,1024]{1,0:T(8,128)(2,1)} %constant_dynamic-update-slice_fusion, s32[]{:T(128)S(6)} %select_n.29, f32[1024]{0:T(1024)S(1)} %bitcast.20), kind=kOutput, calls=%fused_computation.2 | convolution fusion | flops 25770852352 | bytes 18878468 | tf_op jit(solution)/shard_map/dot_general | solution.py:39
  180.8 0.0 copy-done.2
  180.8 3.1 %fusion.4 = f32[2,512,512]{2,1,0:T(8,128)} fusion(f32[512,2,512]{0,2,1:T(8,128)S(1)} %bitcast.15, bf16[64,2,8,512]{3,2,1,0:T(8,128)(2,1)S(1)} %bitcast.18), kind=kOutput, calls=%fused_computation.3 | convolution fusion | flops 3221225472 | bytes 5242880 | tf_op jit(solution)/shard_map/ikc,ikd->ckd/dot_general | solution.py:45
  183.9 2.9 %copy.8 = f32[512,1024]{1,0:T(8,128)} copy(f32[512,1024]{0,1:T(8,128)} %bitcast.17) | data formatting | bytes 4194304 | tf_op jit(solution)/shard_map/reshape | solution.py:49
  186.9 0.0 reduce-scatter.2.cloned.1.call-update
  186.9 1.8 copy.9
  188.7 37.8 %reduce-scatter.2.cloned.1.call-done = f32[64,1024]{1,0:T(8,128)} async-done(((f32[512,1024]{1,0:T(8,128)}), f32[64,1024]{1,0:T(8,128)}) %reduce-scatter.2.cloned.1.call-update) | async-done | bytes 262160 | tf_op jit(solution)/shard_map/reduce_scatter | solution.py:48
  226.4 0.0 copy-done.5
  226.5 1.7 sub.17
  (2 shorter events, 0.0 us)
Async XLA Ops:
  7.2 117.0 %copy-start = (bf16[512,1024]{1,0:T(8,128)(2,1)S(1)}, bf16[512,1024]{1,0:T(8,128)(2,1)}, u32[]{:S(2)}) copy-start(bf16[512,1024]{1,0:T(8,128)(2,1)} %param.6) | copy-start | bytes 3145732
  7.2 154.8 %all-gather.2.cloned.1.call-start = ((), (), s32[]{:S(2)}) async-start(), calls=%async_computation.1 | async-start | bytes 10485760 | tf_op jit(solution)/shard_map/all_gather | solution.py:38
  7.9 218.5 %reduce-scatter.2.cloned.1.call-start = ((), (), s32[]{:S(2)}) async-start(), calls=%async_computation.2 | async-start | bytes 2359296 | tf_op jit(solution)/shard_map/reduce_scatter | solution.py:48
  11.0 15.9 %copy-start.1 = (bf16[512,1024]{1,0:T(8,128)(2,1)}, bf16[512,1024]{1,0:T(8,128)(2,1)S(1)}, u32[]{:S(2)}) copy-start(bf16[512,1024]{1,0:T(8,128)(2,1)S(1)} %broadcast_multiply_fusion) | copy-start | bytes 3145732
  11.0 15.9 %collective-permute-start = (bf16[512,1024]{1,0:T(8,128)(2,1)S(1)}, bf16[512,1024]{1,0:T(8,128)(2,1)S(1)}, u32[]{:S(2)}, u32[]{:S(2)}) collective-permute-start(bf16[512,1024]{1,0:T(8,128)(2,1)S(1)} %broadcast_multiply_fusion), channel_id=1, source_target_pairs={{0,4},{4,8},{8,12},{12,16},{16,20},{20,24},{24,28},{28,0},{1,5},{5... | collective-permute-start | bytes 3145736 | tf_op jit(solution)/shard_map/ppermute | solution.py:15
  26.8 24.6 %collective-permute-start.1 = (bf16[512,1024]{1,0:T(8,128)(2,1)S(1)}, bf16[512,1024]{1,0:T(8,128)(2,1)S(1)}, u32[]{:S(2)}, u32[]{:S(2)}) collective-permute-start(bf16[512,1024]{1,0:T(8,128)(2,1)S(1)} %collective-permute-done), channel_id=1, source_target_pairs={{0,4},{4,8},{8,12},{12,16},{16,20},{20,24},{24,28},{28,0},{1,5},{5... | collective-permute-start | bytes 3145736 | tf_op jit(solution)/shard_map/ppermute | solution.py:15
  26.8 24.6 %collective-permute-start.4 = (bf16[512,1024]{1,0:T(8,128)(2,1)S(1)}, bf16[512,1024]{1,0:T(8,128)(2,1)S(1)}, u32[]{:S(2)}, u32[]{:S(2)}) collective-permute-start(bf16[512,1024]{1,0:T(8,128)(2,1)S(1)} %broadcast_multiply_fusion), channel_id=1, source_target_pairs={{0,28},{4,0},{8,4},{12,8},{16,12},{20,16},{24,20},{28,24},{1,29},{... | collective-permute-start | bytes 3145736 | tf_op jit(solution)/shard_map/ppermute | solution.py:17
  51.4 1.0 copy-start.3
  51.4 25.2 %collective-permute-start.2 = (bf16[512,1024]{1,0:T(8,128)(2,1)S(1)}, bf16[512,1024]{1,0:T(8,128)(2,1)}, u32[]{:S(2)}, u32[]{:S(2)}) collective-permute-start(bf16[512,1024]{1,0:T(8,128)(2,1)S(1)} %collective-permute-done.1), channel_id=1, source_target_pairs={{0,4},{4,8},{8,12},{12,16},{16,20},{20,24},{24,28},{28,0},{1,5},{5... | collective-permute-start | bytes 3145736 | tf_op jit(solution)/shard_map/ppermute | solution.py:15
  52.4 24.2 %collective-permute-start.5 = (bf16[512,1024]{1,0:T(8,128)(2,1)S(1)}, bf16[512,1024]{1,0:T(8,128)(2,1)}, u32[]{:S(2)}, u32[]{:S(2)}) collective-permute-start(bf16[512,1024]{1,0:T(8,128)(2,1)S(1)} %collective-permute-done.4), channel_id=1, source_target_pairs={{0,28},{4,0},{8,4},{12,8},{16,12},{20,16},{24,20},{28,24},{1,29},{... | collective-permute-start | bytes 3145736 | tf_op jit(solution)/shard_map/ppermute | solution.py:17
  76.6 26.0 %collective-permute-start.3 = (bf16[512,1024]{1,0:T(8,128)(2,1)}, bf16[512,1024]{1,0:T(8,128)(2,1)}, u32[]{:S(2)}, u32[]{:S(2)}) collective-permute-start(bf16[512,1024]{1,0:T(8,128)(2,1)} %collective-permute-done.2), channel_id=1, source_target_pairs={{0,4},{4,8},{8,12},{12,16},{16,20},{20,24},{24,28},{28,0},{1,5},{5... | collective-permute-start | bytes 3145736 | tf_op jit(solution)/shard_map/ppermute | solution.py:15
  76.6 45.4 %copy-start.4 = (bf16[512,1024]{1,0:T(8,128)(2,1)S(1)}, bf16[512,1024]{1,0:T(8,128)(2,1)}, u32[]{:S(2)}) copy-start(bf16[512,1024]{1,0:T(8,128)(2,1)} %copy-done.3) | copy-start | bytes 3145732
  76.6 39.7 %collective-permute-start.6 = (bf16[512,1024]{1,0:T(8,128)(2,1)}, bf16[512,1024]{1,0:T(8,128)(2,1)S(1)}, u32[]{:S(2)}, u32[]{:S(2)}) collective-permute-start(bf16[512,1024]{1,0:T(8,128)(2,1)} %collective-permute-done.5), channel_id=1, source_target_pairs={{0,28},{4,0},{8,4},{12,8},{16,12},{20,16},{24,20},{28,24},{1,29},{... | collective-permute-start | bytes 3145736 | tf_op jit(solution)/shard_map/ppermute | solution.py:17
  128.8 52.0 %copy-start.2 = (bf16[512,1024]{1,0:T(8,128)(2,1)S(1)}, bf16[512,1024]{1,0:T(8,128)(2,1)}, u32[]{:S(2)}) copy-start(bf16[512,1024]{1,0:T(8,128)(2,1)} %copy-done.1) | copy-start | bytes 3145732
  129.8 96.6 %copy-start.5 = (f32[64,1024]{1,0:T(8,128)S(1)}, f32[64,1024]{1,0:T(8,128)}, u32[]{:S(2)}) copy-start(f32[64,1024]{1,0:T(8,128)} %param.7) | copy-start | bytes 786436
Sparse Core Ops, SparseCore 0:
  9.6 152.3 all-gather.1
  187.0 39.4 reduce-scatter.1
